TPU v7x, 32 devices: a whole 2x2x4 slice. The times are simulated.
32 devices in a mesh: seq: 8 (over z, y), pass: 4 (over x, core).
Axes of the slice: x: 2, y: 2, z: 4, core: 2. Of those that a mesh axis runs over, the one named last changes fastest.
Arguments:
- x_rows: bfloat16 [4, 8192, 768], P('pass', 'seq'), may hold values from -6 to 6
- pass_depth: int32 [8, 1024], P('seq'), may hold values from 1 to 4
- cotangent: bfloat16 [4, 8192, 768], P('pass', 'seq'), may hold values from -6 to 6
- pass_emb: float32 [4, 768], replicated, may hold values from -3 to 3
- ln1_gain: float32 [768], replicated, may hold values from 0.1 to 1.9
- ln1_bias: float32 [768], replicated, may hold values from -2 to 2
- w_qkv: bfloat16 [768, 2304], P(('seq', 'pass')), may hold values from -0.21875 to 0.21875
- q_bias: float32 [768], replicated, may hold values from -2 to 2
- v_bias: float32 [768], replicated, may hold values from -0.6 to 0.6
- w_out: bfloat16 [768, 768], P(('seq', 'pass')), may hold values from -0.875 to 0.875
- out_bias: float32 [768], replicated, may hold values from -2 to 2
- ln2_gain: float32 [768], replicated, may hold values from 0.1 to 1.9
- ln2_bias: float32 [768], replicated, may hold values from -2 to 2
- w_up: bfloat16 [768, 3072], P(('seq', 'pass')), may hold values from -0.21875 to 0.21875
- up_bias: float32 [3072], replicated, may hold values from -3 to 3
- w_down: bfloat16 [3072, 768], P(('seq', 'pass')), may hold values from -0.109375 to 0.109375
- down_bias: float32 [768], replicated, may hold values from -2 to 2
Outputs:
- out_rows: bfloat16 [4, 8192, 768], P('pass', 'seq')
- x_grad: float32 [4, 8192, 768], P('pass', 'seq')
- w_qkv_grad: float32 [768, 2304], P(('seq', 'pass'))
- q_bias_grad: float32 [768], replicated
- v_bias_grad: float32 [768], replicated
- w_out_grad: float32 [768, 768], P(('seq', 'pass'))
- out_bias_grad: float32 [768], replicated
- ln1_gain_grad: float32 [768], replicated
- ln1_bias_grad: float32 [768], replicated
- ln2_gain_grad: float32 [768], replicated
- ln2_bias_grad: float32 [768], replicated
- w_up_grad: float32 [768, 3072], P(('seq', 'pass'))
- up_bias_grad: float32 [3072], replicated
- w_down_grad: float32 [3072, 768], P(('seq', 'pass'))
- down_bias_grad: float32 [768], replicated
- pass_emb_grad: float32 [4, 768], P('pass')
Inputs may be any that keep to these rules, and one draw needn't show every extreme that they name: A token serves as a key in its first pass_depth passes only; every token counts as a key in pass 0.
All inputs are finite; a program needn't handle non-finite values.
Results may differ from a plain program's by a relative error of at most 0.012.
Values may be sent and summed in bfloat16 or wider, within the bound.
No kernel may reach another device: no remote copies, remote signals or barrier semaphores. Data moves between devices by JAX's collectives and lax.ppermute only.
A program may use at most 256 MiB of HBM per device.

v0:
```python
from functools import partial
import math
import jax
import jax.numpy as jnp
from jax import lax
from jax.sharding import PartitionSpec as P

HEADS = 12
HEAD_DIM = 64
norm_eps = 1e-05


def layer_norm(values, gain_row, shift_row):
    center = values - jnp.mean(values, axis=-1, keepdims=True)
    inverse = lax.rsqrt(jnp.mean(center * center, axis=-1, keepdims=True) + norm_eps)
    return center * inverse * gain_row + shift_row


def gelu_exact(values):
    return jax.nn.gelu(values, approximate=False)


def matmul(first_op, second_op):
    return jnp.dot(first_op, second_op, preferred_element_type=jnp.float32)


def matmul_tn(first_op, second_op):
    return lax.dot_general(
        first_op, second_op, (((0,), (0,)), ((), ())), preferred_element_type=jnp.float32
    )


def matmul_nt(first_op, second_op):
    return lax.dot_general(
        first_op, second_op, (((1,), (1,)), ((), ())), preferred_element_type=jnp.float32
    )


def per_device(
    x_rows,
    pass_depth,
    cotangent,
    pass_emb,
    ln1_gain,
    ln1_bias,
    w_qkv,
    q_bias,
    v_bias,
    w_out,
    out_bias,
    ln2_gain,
    ln2_bias,
    w_up,
    up_bias,
    w_down,
    down_bias,
):
    bfloat = jnp.bfloat16
    model_width = x_rows.shape[2]
    seq_count, seq_len = pass_depth.shape
    passes = lax.axis_size("pass")
    pass_id = lax.axis_index("pass")
    key_total = passes * seq_len
    block_rows = math.gcd(seq_len, 512)
    block_count = seq_len // block_rows
    score_scale = HEAD_DIM ** (-0.5)

    def split_heads(flat_rows, lead_count):
        shaped = flat_rows.reshape(lead_count, seq_count, seq_len, HEADS, HEAD_DIM)
        return shaped.transpose(1, 3, 0, 2, 4).reshape(
            seq_count, HEADS, lead_count * seq_len, HEAD_DIM
        )

    def merge_heads(split_rows, lead_count):
        shaped = split_rows.reshape(seq_count, HEADS, lead_count, seq_len, HEAD_DIM)
        return shaped.transpose(2, 0, 3, 1, 4).reshape(
            lead_count * seq_count * seq_len, HEADS * HEAD_DIM
        )

    full_qkv, full_out, full_up, full_down = (
        lax.all_gather(w_qkv, ("seq", "pass"), axis=0, tiled=True),
        lax.all_gather(w_out, ("seq", "pass"), axis=0, tiled=True),
        lax.all_gather(w_up, ("seq", "pass"), axis=0, tiled=True),
        lax.all_gather(w_down, ("seq", "pass"), axis=0, tiled=True),
    )
    pass_row = lax.dynamic_index_in_dim(pass_emb, pass_id, 0, keepdims=False)
    stream_in = x_rows[0].astype(jnp.float32) + pass_row
    normed_one, norm_one_back = jax.vjp(layer_norm, stream_in, ln1_gain, ln1_bias)
    normed_one = normed_one.astype(bfloat)
    projected = matmul(normed_one, full_qkv)
    queries = (projected[:, :model_width] + q_bias).astype(bfloat)
    key_rows = projected[:, model_width : 2 * model_width].astype(bfloat)
    value_rows = (projected[:, 2 * model_width :] + v_bias).astype(bfloat)
    all_keys, all_values = (
        lax.all_gather(key_rows, "pass", axis=0, tiled=True),
        lax.all_gather(value_rows, "pass", axis=0, tiled=True),
    )
    query_heads = split_heads(queries, 1)
    key_heads = split_heads(all_keys, passes)
    value_heads = split_heads(all_values, passes)
    item_index = jnp.arange(seq_count * HEADS, dtype=jnp.int32)
    item_list = (item_index // HEADS, item_index % HEADS)

    def item_slices(item, kept):
        seq_index, head_index = item
        query_all = lax.dynamic_slice(
            query_heads, (seq_index, head_index, 0, 0), (1, 1, seq_len, HEAD_DIM)
        )[0, 0]
        key_all = lax.dynamic_slice(
            key_heads, (seq_index, head_index, 0, 0), (1, 1, key_total, HEAD_DIM)
        )[0, 0]
        value_all = lax.dynamic_slice(
            value_heads, (seq_index, head_index, 0, 0), (1, 1, key_total, HEAD_DIM)
        )[0, 0]
        key_all = key_all.reshape(passes, seq_len, HEAD_DIM)[:kept]
        value_all = value_all.reshape(passes, seq_len, HEAD_DIM)[:kept]
        depth_row = lax.dynamic_index_in_dim(pass_depth, seq_index, 0, keepdims=False)
        return (query_all, key_all, value_all, depth_row)

    def block_scores(kept, query_all, key_all, value_all, depth_row, block_index):
        end_row = (block_index + 1) * block_rows
        key_part = key_all[:, :end_row].reshape(kept * end_row, HEAD_DIM)
        value_part = value_all[:, :end_row].reshape(kept * end_row, HEAD_DIM)
        key_pass = jnp.repeat(jnp.arange(kept, dtype=jnp.int32), end_row)
        key_pos = jnp.tile(jnp.arange(end_row, dtype=jnp.int32), kept)
        key_valid = key_pass < jnp.tile(depth_row[:end_row], kept)
        query_part = query_all[block_index * block_rows : end_row]
        query_pos = block_index * block_rows + jnp.arange(block_rows, dtype=jnp.int32)
        allowed = key_valid[None, :] & (key_pos[None, :] <= query_pos[:, None])
        raw_scores = matmul_nt(query_part, key_part) * score_scale
        return (query_part, key_part, value_part, jnp.where(allowed, raw_scores, -1e30))

    def attend_kept(kept, item):
        query_all, key_all, value_all, depth_row = item_slices(item, kept)
        outputs = []
        sums = []
        for block_index in range(block_count):
            query_part, key_part, value_part, scores = block_scores(
                kept, query_all, key_all, value_all, depth_row, block_index
            )
            row_max = jnp.max(scores, axis=-1, keepdims=True)
            exp_scores = jnp.exp(scores - row_max)
            row_sum = jnp.sum(exp_scores, axis=-1, keepdims=True)
            prob_low = (exp_scores / row_sum).astype(bfloat)
            outputs.append(matmul(prob_low, value_part).astype(bfloat))
            sums.append(row_max[:, 0] + jnp.log(row_sum[:, 0]))
        return (jnp.concatenate(outputs, axis=0), jnp.concatenate(sums, axis=0))

    def attend(item):
        return lax.switch(
            pass_id, [partial(attend_kept, kept) for kept in range(1, passes + 1)], item
        )

    head_out, log_sums = lax.map(attend, item_list)
    attn_rows = merge_heads(head_out.reshape(seq_count, HEADS, seq_len, HEAD_DIM), 1)
    mixed = stream_in + matmul(attn_rows, full_out) + out_bias
    normed_two, norm_two_back = jax.vjp(layer_norm, mixed, ln2_gain, ln2_bias)
    normed_two = normed_two.astype(bfloat)
    upper = matmul(normed_two, full_up) + up_bias
    activated, gelu_back = jax.vjp(gelu_exact, upper)
    activated = activated.astype(bfloat)
    out_rows = (mixed + matmul(activated, full_down) + down_bias).astype(bfloat)
    full_qkv, full_out, full_up, full_down = (
        lax.all_gather(w_qkv, ("seq", "pass"), axis=0, tiled=True),
        lax.all_gather(w_out, ("seq", "pass"), axis=0, tiled=True),
        lax.all_gather(w_up, ("seq", "pass"), axis=0, tiled=True),
        lax.all_gather(w_down, ("seq", "pass"), axis=0, tiled=True),
    )
    out_grad = cotangent[0].astype(jnp.float32)
    down_low = out_grad.astype(bfloat)
    down_grad = matmul_tn(activated, down_low)
    (upper_grad,) = gelu_back(matmul_nt(down_low, full_down))
    upper_low = upper_grad.astype(bfloat)
    up_grad = matmul_tn(normed_two, upper_low)
    mixed_part, ln2_gain_part, ln2_bias_part = norm_two_back(matmul_nt(upper_low, full_up))
    mixed_grad = out_grad + mixed_part
    proj_low = mixed_grad.astype(bfloat)
    out_weight_grad = matmul_tn(attn_rows, proj_low)
    attn_grad = matmul_nt(proj_low, full_out).astype(bfloat)
    grad_heads = split_heads(attn_grad, 1)

    def attend_back_kept(kept, item_and_sum):
        item, log_sum = item_and_sum
        seq_index, head_index = item
        query_all, key_all, value_all, depth_row = item_slices(item, kept)
        grad_all = lax.dynamic_slice(
            grad_heads, (seq_index, head_index, 0, 0), (1, 1, seq_len, HEAD_DIM)
        )[0, 0]
        key_acc = jnp.zeros((kept, seq_len, HEAD_DIM), jnp.float32)
        value_acc = jnp.zeros((kept, seq_len, HEAD_DIM), jnp.float32)
        query_pieces = []
        for block_index in range(block_count):
            end_row = (block_index + 1) * block_rows
            query_part, key_part, value_part, scores = block_scores(
                kept, query_all, key_all, value_all, depth_row, block_index
            )
            attn_prob = jnp.exp(scores - log_sum[block_index * block_rows : end_row, None])
            grad_part = grad_all[block_index * block_rows : end_row]
            prob_grad = matmul_nt(grad_part, value_part)
            score_grad = (
                attn_prob * (prob_grad - jnp.sum(attn_prob * prob_grad, axis=-1, keepdims=True))
            ).astype(bfloat)
            query_pieces.append(matmul(score_grad, key_part) * score_scale)
            key_term = matmul_tn(score_grad, query_part) * score_scale
            value_term = matmul_tn(attn_prob.astype(bfloat), grad_part)
            key_acc = key_acc.at[:, :end_row].add(key_term.reshape(kept, end_row, HEAD_DIM))
            value_acc = value_acc.at[:, :end_row].add(value_term.reshape(kept, end_row, HEAD_DIM))
        key_full = jnp.zeros((passes, seq_len, HEAD_DIM), jnp.float32).at[:kept].set(key_acc)
        value_full = jnp.zeros((passes, seq_len, HEAD_DIM), jnp.float32).at[:kept].set(value_acc)
        return (
            jnp.concatenate(query_pieces, axis=0),
            key_full.reshape(key_total, HEAD_DIM),
            value_full.reshape(key_total, HEAD_DIM),
        )

    def attend_back(item_and_sum):
        return lax.switch(
            pass_id,
            [partial(attend_back_kept, kept) for kept in range(1, passes + 1)],
            item_and_sum,
        )

    query_grads, key_grads, value_grads = lax.map(attend_back, (item_list, log_sums))

    def whole_rows(per_item):
        return merge_heads(per_item.reshape(seq_count, HEADS, key_total, HEAD_DIM), passes)

    own_keys, own_values = (
        lax.psum_scatter(
            whole_rows(key_grads).astype(jnp.bfloat16), "pass", scatter_dimension=0, tiled=True
        ).astype(jnp.float32),
        lax.psum_scatter(
            whole_rows(value_grads).astype(jnp.bfloat16), "pass", scatter_dimension=0, tiled=True
        ).astype(jnp.float32),
    )
    query_low = merge_heads(query_grads.reshape(seq_count, HEADS, seq_len, HEAD_DIM), 1).astype(
        bfloat
    )
    key_low = own_keys.astype(bfloat)
    value_low = own_values.astype(bfloat)
    qkv_low = jnp.concatenate([query_low, key_low, value_low], axis=1)
    qkv_grad = matmul_tn(normed_one, qkv_low)
    stream_part, ln1_gain_part, ln1_bias_part = norm_one_back(matmul_nt(qkv_low, full_qkv))
    stream_grad = mixed_grad + stream_part
    pass_select = (jnp.arange(passes, dtype=jnp.int32) == pass_id).astype(jnp.float32)
    pass_part = pass_select[:, None] * jnp.sum(stream_grad, axis=0)[None, :]
    shard_qkv, shard_out, shard_up, shard_down = (
        lax.psum_scatter(qkv_grad, ("seq", "pass"), scatter_dimension=0, tiled=True),
        lax.psum_scatter(out_weight_grad, ("seq", "pass"), scatter_dimension=0, tiled=True),
        lax.psum_scatter(up_grad, ("seq", "pass"), scatter_dimension=0, tiled=True),
        lax.psum_scatter(down_grad, ("seq", "pass"), scatter_dimension=0, tiled=True),
    )
    (
        gain_one,
        shift_one,
        query_bias_sum,
        value_bias_sum,
        out_bias_sum,
        gain_two,
        shift_two,
        up_bias_sum,
        down_bias_sum,
        pass_total,
    ) = lax.psum(
        (
            ln1_gain_part,
            ln1_bias_part,
            jnp.sum(query_low.astype(jnp.float32), axis=0),
            jnp.sum(value_low.astype(jnp.float32), axis=0),
            jnp.sum(mixed_grad, axis=0),
            ln2_gain_part,
            ln2_bias_part,
            jnp.sum(upper_low.astype(jnp.float32), axis=0),
            jnp.sum(out_grad, axis=0),
            pass_part,
        ),
        ("seq", "pass"),
    )
    pass_grad = lax.dynamic_slice_in_dim(pass_total, pass_id, 1, 0)
    return (
        out_rows[None],
        stream_grad[None],
        shard_qkv,
        query_bias_sum,
        value_bias_sum,
        shard_out,
        out_bias_sum,
        gain_one,
        shift_one,
        gain_two,
        shift_two,
        shard_up,
        up_bias_sum,
        shard_down,
        down_bias_sum,
        pass_grad,
    )


def solution(mesh):
    placed = (
        P("pass", "seq", None),
        P("seq", None),
        P("pass", "seq", None),
        P(),
        P(),
        P(),
        P(("seq", "pass"), None),
        P(),
        P(),
        P(("seq", "pass"), None),
        P(),
        P(),
        P(),
        P(("seq", "pass"), None),
        P(),
        P(("seq", "pass"), None),
        P(),
    )
    return jax.shard_map(
        per_device,
        mesh=mesh,
        in_specs=placed,
        out_specs=(
            P("pass", "seq", None),
            P("pass", "seq", None),
            P(("seq", "pass"), None),
            P(),
            P(),
            P(("seq", "pass"), None),
            P(),
            P(),
            P(),
            P(),
            P(),
            P(("seq", "pass"), None),
            P(),
            P(("seq", "pass"), None),
            P(),
            P("pass", None),
        ),
        check_vma=False,
    )
```

profile of v0, /device:TPU:0, one launch (start us, length us, event | category | flops | bytes accessed | tf_op | source)
XLA Modules:
  0.0 2400.3 jit_solution(17493814154461534555)
XLA Ops:
  10.8 62.9 %all-gather.7.cloned.1.call-done = bf16[768,2304]{1,0:T(8,128)(2,1)} async-done(((bf16[24,2304]{1,0:T(8,128)(2,1)}), bf16[768,2304]{1,0:T(8,128)(2,1)}) %all-gather.7.cloned.1.call-update) | async-done | bytes 3538960 | tf_op jit(solution)/shard_map/all_gather | solution.py:81
  73.7 6.5 fusion.213
  84.4 3.3 slice.922
  94.8 35.0 %all-gather.11.cloned.1.call-done = bf16[4096,768]{1,0:T(8,128)(2,1)} async-done(((bf16[1024,768]{1,0:T(8,128)(2,1)}), bf16[4096,768]{1,0:T(8,128)(2,1)}) %all-gather.11.cloned.1.call-update) | async-done | bytes 6291472 | tf_op jit(solution)/shard_map/all_gather | solution.py:96
  129.7 8.8 copy.69
  138.5 11.4 reshape.1447
  150.0 14.1 copy.91
  164.1 13.6 all-gather.9.cloned.1.call-done
  177.7 8.8 copy.68
  186.5 11.2 reshape.1445
  197.7 14.2 copy.90
  212.4 155.0 %while.64 = (s32[]{:T(128)}, bf16[12,1024,64]{1,2,0:T(8,128)(2,1)}, f32[12,1024]{1,0:T(8,128)}, s32[12]{0:T(128)}, s32[1,1024]{1,0:T(1,128)S(1)}, /*index=5*/bf1...) while((s32[]{:T(128)}, bf16[12,1024,64]{1,2,0:T(8,128)(2,1)}, ...), condition=%wide.region_23.24_spmd, body=%wide.region_2.23_spmd.sunk | while | flops 837097984 | bytes 77652256 | solution.py:154
  213.9 8.8 conditional.4
  226.0 8.8 conditional.4
  238.1 8.8 conditional.4
  250.2 8.8 conditional.4
  262.4 8.8 conditional.4
  274.5 8.8 conditional.4
  286.6 8.8 conditional.4
  298.7 8.8 conditional.4
  310.9 8.8 conditional.4
  323.0 8.8 conditional.4
  335.1 8.8 conditional.4
  347.2 8.8 conditional.4
  367.4 4.0 fusion.229
  372.2 38.4 %multiply_convert_fusion.8 = (bf16[1024,3072]{1,0:T(8,128)(2,1)}, f32[1024,3072]{1,0:T(8,128)}, f32[1024,3072]{1,0:T(8,128)}) fusion(f32[3072]{0:T(1024)S(1)} %copy-done.58, bf16[768,3072]{1,0:T(8,128)(2,1)} %all-gather.15.cloned.1.call-done, f32[1024,768]{0,1:T(8,128)S(1)} %get-tuple-element.1126, f32[768]{0:T(1024)S(1)} %copy-done.59, ...), kind=kOutput, calls=%fused_computation.371 | convolution fusion | flops 5043388416 | bytes 39348224 | tf_op jit(solution)/shard_map/dot_general | solution.py:24
  410.6 19.0 convert_reduce_fusion
  429.6 10.3 fusion.231
  440.0 3.5 copy.75
  453.3 448.2 %while.65 = (s32[]{:T(128)}, bf16[12,1024,64]{1,2,0:T(8,128)(2,1)}, bf16[12,4096,64]{1,2,0:T(8,128)(2,1)}, bf16[12,4096,64]{1,2,0:T(8,128)(2,1)}, s32[12]{0:T(12...) while((s32[]{:T(128)}, bf16[12,1024,64]{1,2,0:T(8,128)(2,1)}, ...), condition=%wide.region_41.42_spmd, body=%wide.region_28.41_spmd.sunk | while | flops 2081166848 | bytes 146125840 | solution.py:223
  455.5 43.3 %conditional.5 = (bf16[1,1024,64]{1,2,0:T(8,128)(2,1)}, bf16[1,4096,64]{1,2,0:T(8,128)(2,1)}, bf16[1,4096,64]{1,2,0:T(8,128)(2,1)}) conditional(s32[]{:T(128)} %get-tuple-element.1366, (s32[1,1024]{1,0:T(1,128)S(1)}, s32[]{:T(128)}, bf16[1,12,1024,64]{3,2,1,0:T(8,128)(2,1)}, bf16[1,12,4096,64]{3,2,1,0:T(8,128)(2,1)}, ...), branch_computations={%region_29.31_spmd, %region_32.34_spmd, %region_35.37_spmd, %regio... | conditional | flops 2081166848 | bytes 143756960 | solution.py:217
  459.2 3.1 copy.65
  505.4 30.0 %conditional.5 = (bf16[1,1024,64]{1,2,0:T(8,128)(2,1)}, bf16[1,4096,64]{1,2,0:T(8,128)(2,1)}, bf16[1,4096,64]{1,2,0:T(8,128)(2,1)}) conditional(s32[]{:T(128)} %get-tuple-element.1366, (s32[1,1024]{1,0:T(1,128)S(1)}, s32[]{:T(128)}, bf16[1,12,1024,64]{3,2,1,0:T(8,128)(2,1)}, bf16[1,12,4096,64]{3,2,1,0:T(8,128)(2,1)}, ...), branch_computations={%region_29.31_spmd, %region_32.34_spmd, %region_35.37_spmd, %regio... | conditional | flops 2081166848 | bytes 143756960 | solution.py:217
  541.2 29.7 %conditional.5 = (bf16[1,1024,64]{1,2,0:T(8,128)(2,1)}, bf16[1,4096,64]{1,2,0:T(8,128)(2,1)}, bf16[1,4096,64]{1,2,0:T(8,128)(2,1)}) conditional(s32[]{:T(128)} %get-tuple-element.1366, (s32[1,1024]{1,0:T(1,128)S(1)}, s32[]{:T(128)}, bf16[1,12,1024,64]{3,2,1,0:T(8,128)(2,1)}, bf16[1,12,4096,64]{3,2,1,0:T(8,128)(2,1)}, ...), branch_computations={%region_29.31_spmd, %region_32.34_spmd, %region_35.37_spmd, %regio... | conditional | flops 2081166848 | bytes 143756960 | solution.py:217
  544.9 3.1 copy.65
  576.6 29.7 %conditional.5 = (bf16[1,1024,64]{1,2,0:T(8,128)(2,1)}, bf16[1,4096,64]{1,2,0:T(8,128)(2,1)}, bf16[1,4096,64]{1,2,0:T(8,128)(2,1)}) conditional(s32[]{:T(128)} %get-tuple-element.1366, (s32[1,1024]{1,0:T(1,128)S(1)}, s32[]{:T(128)}, bf16[1,12,1024,64]{3,2,1,0:T(8,128)(2,1)}, bf16[1,12,4096,64]{3,2,1,0:T(8,128)(2,1)}, ...), branch_computations={%region_29.31_spmd, %region_32.34_spmd, %region_35.37_spmd, %regio... | conditional | flops 2081166848 | bytes 143756960 | solution.py:217
  612.1 29.7 %conditional.5 = (bf16[1,1024,64]{1,2,0:T(8,128)(2,1)}, bf16[1,4096,64]{1,2,0:T(8,128)(2,1)}, bf16[1,4096,64]{1,2,0:T(8,128)(2,1)}) conditional(s32[]{:T(128)} %get-tuple-element.1366, (s32[1,1024]{1,0:T(1,128)S(1)}, s32[]{:T(128)}, bf16[1,12,1024,64]{3,2,1,0:T(8,128)(2,1)}, bf16[1,12,4096,64]{3,2,1,0:T(8,128)(2,1)}, ...), branch_computations={%region_29.31_spmd, %region_32.34_spmd, %region_35.37_spmd, %regio... | conditional | flops 2081166848 | bytes 143756960 | solution.py:217
  647.6 29.7 %conditional.5 = (bf16[1,1024,64]{1,2,0:T(8,128)(2,1)}, bf16[1,4096,64]{1,2,0:T(8,128)(2,1)}, bf16[1,4096,64]{1,2,0:T(8,128)(2,1)}) conditional(s32[]{:T(128)} %get-tuple-element.1366, (s32[1,1024]{1,0:T(1,128)S(1)}, s32[]{:T(128)}, bf16[1,12,1024,64]{3,2,1,0:T(8,128)(2,1)}, bf16[1,12,4096,64]{3,2,1,0:T(8,128)(2,1)}, ...), branch_computations={%region_29.31_spmd, %region_32.34_spmd, %region_35.37_spmd, %regio... | conditional | flops 2081166848 | bytes 143756960 | solution.py:217
  683.0 29.7 %conditional.5 = (bf16[1,1024,64]{1,2,0:T(8,128)(2,1)}, bf16[1,4096,64]{1,2,0:T(8,128)(2,1)}, bf16[1,4096,64]{1,2,0:T(8,128)(2,1)}) conditional(s32[]{:T(128)} %get-tuple-element.1366, (s32[1,1024]{1,0:T(1,128)S(1)}, s32[]{:T(128)}, bf16[1,12,1024,64]{3,2,1,0:T(8,128)(2,1)}, bf16[1,12,4096,64]{3,2,1,0:T(8,128)(2,1)}, ...), branch_computations={%region_29.31_spmd, %region_32.34_spmd, %region_35.37_spmd, %regio... | conditional | flops 2081166848 | bytes 143756960 | solution.py:217
  718.5 29.7 %conditional.5 = (bf16[1,1024,64]{1,2,0:T(8,128)(2,1)}, bf16[1,4096,64]{1,2,0:T(8,128)(2,1)}, bf16[1,4096,64]{1,2,0:T(8,128)(2,1)}) conditional(s32[]{:T(128)} %get-tuple-element.1366, (s32[1,1024]{1,0:T(1,128)S(1)}, s32[]{:T(128)}, bf16[1,12,1024,64]{3,2,1,0:T(8,128)(2,1)}, bf16[1,12,4096,64]{3,2,1,0:T(8,128)(2,1)}, ...), branch_computations={%region_29.31_spmd, %region_32.34_spmd, %region_35.37_spmd, %regio... | conditional | flops 2081166848 | bytes 143756960 | solution.py:217
  753.9 29.7 %conditional.5 = (bf16[1,1024,64]{1,2,0:T(8,128)(2,1)}, bf16[1,4096,64]{1,2,0:T(8,128)(2,1)}, bf16[1,4096,64]{1,2,0:T(8,128)(2,1)}) conditional(s32[]{:T(128)} %get-tuple-element.1366, (s32[1,1024]{1,0:T(1,128)S(1)}, s32[]{:T(128)}, bf16[1,12,1024,64]{3,2,1,0:T(8,128)(2,1)}, bf16[1,12,4096,64]{3,2,1,0:T(8,128)(2,1)}, ...), branch_computations={%region_29.31_spmd, %region_32.34_spmd, %region_35.37_spmd, %regio... | conditional | flops 2081166848 | bytes 143756960 | solution.py:217
  789.3 29.7 %conditional.5 = (bf16[1,1024,64]{1,2,0:T(8,128)(2,1)}, bf16[1,4096,64]{1,2,0:T(8,128)(2,1)}, bf16[1,4096,64]{1,2,0:T(8,128)(2,1)}) conditional(s32[]{:T(128)} %get-tuple-element.1366, (s32[1,1024]{1,0:T(1,128)S(1)}, s32[]{:T(128)}, bf16[1,12,1024,64]{3,2,1,0:T(8,128)(2,1)}, bf16[1,12,4096,64]{3,2,1,0:T(8,128)(2,1)}, ...), branch_computations={%region_29.31_spmd, %region_32.34_spmd, %region_35.37_spmd, %regio... | conditional | flops 2081166848 | bytes 143756960 | solution.py:217
  824.8 29.7 %conditional.5 = (bf16[1,1024,64]{1,2,0:T(8,128)(2,1)}, bf16[1,4096,64]{1,2,0:T(8,128)(2,1)}, bf16[1,4096,64]{1,2,0:T(8,128)(2,1)}) conditional(s32[]{:T(128)} %get-tuple-element.1366, (s32[1,1024]{1,0:T(1,128)S(1)}, s32[]{:T(128)}, bf16[1,12,1024,64]{3,2,1,0:T(8,128)(2,1)}, bf16[1,12,4096,64]{3,2,1,0:T(8,128)(2,1)}, ...), branch_computations={%region_29.31_spmd, %region_32.34_spmd, %region_35.37_spmd, %regio... | conditional | flops 2081166848 | bytes 143756960 | solution.py:217
  860.3 29.7 %conditional.5 = (bf16[1,1024,64]{1,2,0:T(8,128)(2,1)}, bf16[1,4096,64]{1,2,0:T(8,128)(2,1)}, bf16[1,4096,64]{1,2,0:T(8,128)(2,1)}) conditional(s32[]{:T(128)} %get-tuple-element.1366, (s32[1,1024]{1,0:T(1,128)S(1)}, s32[]{:T(128)}, bf16[1,12,1024,64]{3,2,1,0:T(8,128)(2,1)}, bf16[1,12,4096,64]{3,2,1,0:T(8,128)(2,1)}, ...), branch_computations={%region_29.31_spmd, %region_32.34_spmd, %region_35.37_spmd, %regio... | conditional | flops 2081166848 | bytes 143756960 | solution.py:217
  901.5 11.2 convert_element_type.251
  912.7 9.5 copy.108
  922.3 11.2 convert_element_type.255
  933.4 9.5 copy.109
  943.0 5.4 fusion.202
  948.6 10.8 fusion.210
  960.8 10.2 fusion.196
  971.0 847.5 %reduce-scatter.7.cloned.1.call-done = bf16[1024,768]{0,1:T(8,128)(2,1)} async-done(((bf16[4096,768]{0,1:T(8,128)(2,1)}), bf16[1024,768]{0,1:T(8,128)(2,1)}) %reduce-scatter.7.cloned.1.call-update) | async-done | bytes 1572880 | tf_op jit(solution)/shard_map/reduce_scatter | solution.py:229
  1818.6 61.1 %reduce-scatter.9.cloned.1.call-done = bf16[1024,768]{0,1:T(8,128)(2,1)} async-done(((bf16[4096,768]{0,1:T(8,128)(2,1)}), bf16[1024,768]{0,1:T(8,128)(2,1)}) %reduce-scatter.9.cloned.1.call-update) | async-done | bytes 1572880 | tf_op jit(solution)/shard_map/reduce_scatter | solution.py:232
  1879.7 9.0 fusion.194
  1889.4 10.3 fusion.199
  1902.3 8.6 fusion.230
  1910.9 3.6 copy.80
  1919.2 3.3 fusion.200
  1922.6 3.7 copy.84
  1926.7 41.1 %all-reduce.14 = (f32[768]{0:T(1024)}, f32[768]{0:T(1024)}, f32[768]{0:T(1024)}, f32[768]{0:T(1024)}, f32[768]{0:T(1024)}, /*index=5*/f32[768]{0:T(1024)}, f32[7...) all-reduce(f32[768]{0:T(1024)S(1)} %reduce_sum.365, ...), channel_id=1, replica_groups=mesh['seq'=8,'pass'=4] {'seq','pass'}, use_global_device_ids=true, to_apply=%region_48.49 | all-reduce | flops 12288 | bytes 98304 | tf_op jit(solution)/shard_map/psum | solution.py:264
  1968.4 16.3 reduce-scatter.13.cloned.1.call-done
  1984.7 141.8 %reduce-scatter.15.cloned.1.call-done = f32[24,3072]{1,0:T(8,128)} async-done(((f32[768,3072]{1,0:T(8,128)}), f32[24,3072]{1,0:T(8,128)}) %reduce-scatter.15.cloned.1.call-update) | async-done | bytes 294928 | tf_op jit(solution)/shard_map/reduce_scatter | solution.py:250
  2126.5 141.0 %reduce-scatter.17.cloned.1.call-done = f32[96,768]{1,0:T(8,128)} async-done(((f32[3072,768]{1,0:T(8,128)}), f32[96,768]{1,0:T(8,128)}) %reduce-scatter.17.cloned.1.call-update) | async-done | bytes 294928 | tf_op jit(solution)/shard_map/reduce_scatter | solution.py:251
  2267.5 125.5 %reduce-scatter.11.cloned.1.call-done = f32[24,2304]{1,0:T(8,128)} async-done(((f32[768,2304]{1,0:T(8,128)}), f32[24,2304]{1,0:T(8,128)}) %reduce-scatter.11.cloned.1.call-update) | async-done | bytes 221200 | tf_op jit(solution)/shard_map/reduce_scatter | solution.py:248
  (922 shorter events, 552.0 us)
Async XLA Ops:
  7.2 66.5 %all-gather.7.cloned.1.call-start = ((), (), s32[]{:S(2)}) async-start(), calls=%async_computation.6 | async-start | bytes 3649536 | tf_op jit(solution)/shard_map/all_gather | solution.py:81
  7.9 121.8 %all-gather.11.cloned.1.call-start = ((), (), s32[]{:S(2)}) async-start(), calls=%async_computation.8 | async-start | bytes 7864320 | tf_op jit(solution)/shard_map/all_gather | solution.py:96
  8.0 65.7 %copy-start.41 = (f32[768]{0:T(1024)S(1)}, f32[768]{0:T(1024)}, u32[]{:S(2)}) copy-start(f32[768]{0:T(1024)} %param.101) | copy-start | bytes 9220
  8.0 65.7 %copy-start.61 = (f32[768]{0:T(1024)S(1)}, f32[768]{0:T(1024)}, u32[]{:S(2)}) copy-start(f32[768]{0:T(1024)} %param.102) | copy-start | bytes 9220
  9.7 70.5 %copy-start.16 = (bf16[1,1024,768]{1,2,0:T(8,128)(2,1)}, bf16[1,1024,768]{1,2,0:T(8,128)(2,1)S(1)}, u32[]{:S(2)}) copy-start(bf16[1,1024,768]{1,2,0:T(8,128)(2,1)S(1)} %copy.66) | copy-start | bytes 4718596
  9.8 63.9 %copy-start.35 = (f32[768]{0:T(1024)}, f32[768]{0:T(1024)S(1)}, u32[]{:S(2)}) copy-start(f32[768]{0:T(1024)S(1)} %dynamic-slice_reduce_fusion) | copy-start | bytes 9220
  10.2 70.0 %copy-start.37 = (f32[1024]{0:T(1024)}, f32[1024]{0:T(1024)S(1)}, u32[]{:S(2)}) copy-start(f32[1024]{0:T(1024)S(1)} %broadcast_multiply_fusion.2) | copy-start | bytes 12292
  10.8 69.4 %copy-start.47 = (f32[1024]{0:T(1024)}, f32[1024]{0:T(1024)S(1)}, u32[]{:S(2)}) copy-start(f32[1024]{0:T(1024)S(1)} %fusion.191) | copy-start | bytes 12292
  10.8 69.4 %copy-start.43 = (f32[1024]{0:T(1024)}, f32[1024]{0:T(1024)S(1)}, u32[]{:S(2)}) copy-start(f32[1024]{0:T(1024)S(1)} %fusion.205) | copy-start | bytes 12292
  10.8 69.4 %copy-start.54 = (f32[768]{0:T(1024)S(1)}, f32[768]{0:T(1024)}, u32[]{:S(2)}) copy-start(f32[768]{0:T(1024)} %param.105) | copy-start | bytes 9220
  10.8 69.4 %copy-start.55 = (f32[768]{0:T(1024)S(1)}, f32[768]{0:T(1024)}, u32[]{:S(2)}) copy-start(f32[768]{0:T(1024)} %param.104) | copy-start | bytes 9220
  80.3 4.1 copy-start.28
  84.4 5.3 copy-start.30
  84.4 93.3 %all-gather.9.cloned.1.call-start = ((), (), s32[]{:S(2)}) async-start(), calls=%async_computation.7 | async-start | bytes 7864320 | tf_op jit(solution)/shard_map/all_gather | solution.py:95
  87.8 279.6 %all-gather.13.cloned.1.call-start = ((), (), s32[]{:S(2)}) async-start(), calls=%async_computation.9 | async-start | bytes 1216512 | tf_op jit(solution)/shard_map/all_gather | solution.py:82
  88.4 283.6 %all-gather.15.cloned.1.call-start = ((), (), s32[]{:S(2)}) async-start(), calls=%async_computation.10 | async-start | bytes 4866048 | tf_op jit(solution)/shard_map/all_gather | solution.py:83
  88.9 321.7 %all-gather.17.cloned.1.call-start = ((), (), s32[]{:S(2)}) async-start(), calls=%async_computation.11 | async-start | bytes 4866048 | tf_op jit(solution)/shard_map/all_gather | solution.py:84
  89.5 1729.0 %reduce-scatter.7.cloned.1.call-start = ((), (), s32[]{:S(2)}) async-start(), calls=%async_computation.12 | async-start | bytes 7864320 | tf_op jit(solution)/shard_map/reduce_scatter | solution.py:229
  197.7 14.7 copy-start.24
  371.4 76.8 %copy-start.20 = (f32[1024,768]{0,1:T(8,128)}, f32[1024,768]{0,1:T(8,128)S(1)}, u32[]{:S(2)}) copy-start(f32[1024,768]{0,1:T(8,128)S(1)} %get-tuple-element.1126) | copy-start | bytes 9437188
  371.5 76.8 %copy-start.39 = (f32[1024]{0:T(1024)}, f32[1024]{0:T(1024)S(1)}, u32[]{:S(2)}) copy-start(f32[1024]{0:T(1024)S(1)} %broadcast_multiply_fusion.1) | copy-start | bytes 12292
  371.9 76.4 %copy-start.45 = (f32[1024]{0:T(1024)}, f32[1024]{0:T(1024)S(1)}, u32[]{:S(2)}) copy-start(f32[1024]{0:T(1024)S(1)} %fusion.206) | copy-start | bytes 12292
  462.2 4.2 copy-start.9
  470.1 6.3 copy-start.13
  512.1 4.2 copy-start.9
  520.0 6.3 copy-start.13
  547.9 4.2 copy-start.9
  555.8 6.3 copy-start.13
  583.4 4.2 copy-start.9
  591.2 6.3 copy-start.13
  618.8 4.2 copy-start.9
  626.7 6.3 copy-start.13
  654.3 4.2 copy-start.9
  662.2 6.3 copy-start.13
  689.8 4.2 copy-start.9
  697.6 6.3 copy-start.13
  725.2 4.2 copy-start.9
  733.1 6.3 copy-start.13
  760.7 4.2 copy-start.9
  768.5 6.3 copy-start.13
  796.1 4.2 copy-start.9
  803.9 6.3 copy-start.13
  831.6 4.2 copy-start.9
  839.4 6.3 copy-start.13
  867.0 4.2 copy-start.9
  874.9 6.3 copy-start.13
  922.2 957.4 %reduce-scatter.9.cloned.1.call-start = ((), (), s32[]{:S(2)}) async-start(), calls=%async_computation.13 | async-start | bytes 7864320 | tf_op jit(solution)/shard_map/reduce_scatter | solution.py:232
  942.9 5.6 copy-start.21
  942.9 5.6 copy-start.40
  943.0 5.6 copy-start.46
  943.0 5.6 copy-start.50
  943.0 5.6 copy-start.60
  943.0 1041.7 %reduce-scatter.13.cloned.1.call-start = ((), (), s32[]{:S(2)}) async-start(), calls=%async_computation.15 | async-start | bytes 2433024 | tf_op jit(solution)/shard_map/reduce_scatter | solution.py:249
  948.5 1178.0 %reduce-scatter.15.cloned.1.call-start = ((), (), s32[]{:S(2)}) async-start(), calls=%async_computation.16 | async-start | bytes 9732096 | tf_op jit(solution)/shard_map/reduce_scatter | solution.py:250
  959.4 1308.1 %reduce-scatter.17.cloned.1.call-start = ((), (), s32[]{:S(2)}) async-start(), calls=%async_computation.17 | async-start | bytes 9732096 | tf_op jit(solution)/shard_map/reduce_scatter | solution.py:251
  970.9 908.7 %copy-start.17 = (bf16[1,1024,768]{1,2,0:T(8,128)(2,1)S(1)}, bf16[1,1024,768]{1,2,0:T(8,128)(2,1)}, u32[]{:S(2)}) copy-start(bf16[1,1024,768]{1,2,0:T(8,128)(2,1)} %copy-done.16) | copy-start | bytes 4718596
  970.9 908.7 %copy-start.32 = (bf16[12,1024,64]{1,2,0:T(8,128)(2,1)S(1)}, bf16[12,1024,64]{1,2,0:T(8,128)(2,1)}, u32[]{:S(2)}) copy-start(bf16[12,1024,64]{1,2,0:T(8,128)(2,1)} %get-tuple-element.909) | copy-start | bytes 4718596
  970.9 908.7 %copy-start.36 = (f32[768]{0:T(1024)S(1)}, f32[768]{0:T(1024)}, u32[]{:S(2)}) copy-start(f32[768]{0:T(1024)} %copy-done.35) | copy-start | bytes 9220
  970.9 908.7 %copy-start.38 = (f32[1024]{0:T(1024)S(1)}, f32[1024]{0:T(1024)}, u32[]{:S(2)}) copy-start(f32[1024]{0:T(1024)} %copy-done.37) | copy-start | bytes 12292
  970.9 908.7 %copy-start.42 = (f32[768]{0:T(1024)S(1)}, f32[768]{0:T(1024)}, u32[]{:S(2)}) copy-start(f32[768]{0:T(1024)} %param.101) | copy-start | bytes 9220
  970.9 908.7 %copy-start.44 = (f32[1024]{0:T(1024)S(1)}, f32[1024]{0:T(1024)}, u32[]{:S(2)}) copy-start(f32[1024]{0:T(1024)} %copy-done.43) | copy-start | bytes 12292
  971.0 908.7 %copy-start.62 = (f32[768]{0:T(1024)S(1)}, f32[768]{0:T(1024)}, u32[]{:S(2)}) copy-start(f32[768]{0:T(1024)} %param.102) | copy-start | bytes 9220
  971.0 1422.0 %reduce-scatter.11.cloned.1.call-start = ((), (), s32[]{:S(2)}) async-start(), calls=%async_computation.14 | async-start | bytes 7299072 | tf_op jit(solution)/shard_map/reduce_scatter | solution.py:248
  1922.6 470.4 %copy-start.1 = (f32[4,768]{1,0:T(4,128)S(1)}, f32[4,768]{1,0:T(4,128)}, u32[]{:S(2)}) copy-start(f32[4,768]{1,0:T(4,128)} %param.100) | copy-start | bytes 36868
  (102 other events, 212.6 us)
Sparse Core Ops, SparseCore 0:
  10.9 62.7 all-gather.6
  84.5 45.1 all-gather.10
  131.3 46.3 all-gather.8
  180.5 54.0 all-gather.12
  237.3 62.5 all-gather.14
  302.7 62.5 all-gather.16
  922.3 896.1 reduce-scatter.6
  1821.3 58.3 reduce-scatter.8
  1885.5 99.1 reduce-scatter.12
  1992.0 134.4 reduce-scatter.14
  2133.0 134.4 reduce-scatter.16
  2274.5 118.4 reduce-scatter.10
where the time goes:
time: 2420 us; the launch traced here: 2400 us
  waiting for transfers between devices  1450 us (60%)
  local copies, waits for them, and re-layouts  426 us (18%)
  matrix products  328 us (14%)
  loops' own time  81.3 us (3%)
  other arithmetic  60.7 us (3%)
  blocking collectives  41.1 us (2%)
    reduce_scatter x1, waiting for transfers between devices, per_device(): lax.psum_scatter(whole_rows(key_grads).astype(jnp.bfloat16), 'pass', scat...  848 us
    reduce_scatter x1, waiting for transfers between devices, per_device(): lax.psum_scatter(up_grad, ('seq', 'pass'), scatter_dimension=0, tiled=True)  142 us
    reduce_scatter x1, waiting for transfers between devices, per_device(): lax.psum_scatter(down_grad, ('seq', 'pass'), scatter_dimension=0, tiled=T...  141 us
    dot_general x76, matrix products, matmul_nt(): lax.dot_general(first_op, second_op, (((1,), (1,)), ((), ())), preferred_...  140 us
    reduce_scatter x1, waiting for transfers between devices, per_device(): lax.psum_scatter(qkv_grad, ('seq', 'pass'), scatter_dimension=0, tiled=True)  126 us
    dot_general x52, matrix products, matmul(): return jnp.dot(first_op, second_op, preferred_element_type=jnp.float32)  102 us
    dot_general x52, matrix products, matmul_tn(): lax.dot_general(first_op, second_op, (((0,), (0,)), ((), ())), preferred_...  85.9 us
    all_gather x1, waiting for transfers between devices, per_device(): lax.all_gather(w_qkv, ('seq', 'pass'), axis=0, tiled=True)  62.9 us
  transfers between devices with their start and end apart: 12, of which 9 were waited for; matrix products, arithmetic and copies ran while one was open for 14% of the time, Pallas kernels for 0%

commit v1 on v0

--- a/solution.py
+++ b/solution.py
@@ -8,6 +8,18 @@
 HEADS = 12
 HEAD_DIM = 64
 norm_eps = 1e-05
+
+
+def collect(x, axis, dim):
+    ways, here, step = (lax.axis_size(axis), lax.axis_index(axis), x.shape[dim])
+    line, have = (x, 1)
+    while have < ways:
+        line = jnp.concatenate(
+            [line, lax.ppermute(line, axis, [(d, (d - have) % ways) for d in range(ways)])],
+            axis=dim,
+        )
+        have = 2 * have
+    return jnp.roll(line, here * step, axis=dim)
 
 
 def layer_norm(values, gain_row, shift_row):
@@ -78,7 +90,7 @@
         )
 
     full_qkv, full_out, full_up, full_down = (
-        lax.all_gather(w_qkv, ("seq", "pass"), axis=0, tiled=True),
+        collect(w_qkv, ("seq", "pass"), 0),
         lax.all_gather(w_out, ("seq", "pass"), axis=0, tiled=True),
         lax.all_gather(w_up, ("seq", "pass"), axis=0, tiled=True),
         lax.all_gather(w_down, ("seq", "pass"), axis=0, tiled=True),

time: 2420 us -> 2560 us (1.058)
  waiting for transfers between devices: 1450 us -> 1550 us
    ppermute x0 -> x5, waiting for transfers between devices: none -> 111 us  [collect(): lax.ppermute(line, axis, [(d, (d - have) % ways) for d in range(ways)])]
  transfers between devices with their start and end apart: 12 -> 17, of which waited for: 9 -> 14; matrix products, arithmetic and copies ran while one was open for 14% -> 14% of each run, Pallas kernels for 0% -> 0%
where the time goes in v1:
time: 2560 us; the launch traced here: 2540 us
  waiting for transfers between devices  1550 us (61%)
  local copies, waits for them, and re-layouts  440 us (17%)
  matrix products  328 us (13%)
  loops' own time  82.6 us (3%)
  other arithmetic  70.9 us (3%)
  blocking collectives  40.5 us (2%)
    reduce_scatter x1, waiting for transfers between devices, per_device(): lax.psum_scatter(whole_rows(key_grads).astype(jnp.bfloat16), 'pass', scat...  839 us
    reduce_scatter x1, waiting for transfers between devices, per_device(): lax.psum_scatter(up_grad, ('seq', 'pass'), scatter_dimension=0, tiled=True)  142 us
    reduce_scatter x1, waiting for transfers between devices, per_device(): lax.psum_scatter(down_grad, ('seq', 'pass'), scatter_dimension=0, tiled=T...  141 us
    dot_general x76, matrix products, matmul_nt(): lax.dot_general(first_op, second_op, (((1,), (1,)), ((), ())), preferred_...  140 us
    reduce_scatter x1, waiting for transfers between devices, per_device(): lax.psum_scatter(qkv_grad, ('seq', 'pass'), scatter_dimension=0, tiled=True)  125 us
    ppermute x5, waiting for transfers between devices, collect(): lax.ppermute(line, axis, [(d, (d - have) % ways) for d in range(ways)])  111 us
    dot_general x52, matrix products, matmul(): return jnp.dot(first_op, second_op, preferred_element_type=jnp.float32)  102 us
    dot_general x52, matrix products, matmul_tn(): lax.dot_general(first_op, second_op, (((0,), (0,)), ((), ())), preferred_...  85.8 us
  transfers between devices with their start and end apart: 17, of which 14 were waited for; matrix products, arithmetic and copies ran while one was open for 14% of the time, Pallas kernels for 0%

profile of v1, /device:TPU:0, one launch (start us, length us, event | category | flops | bytes accessed | tf_op | source)
XLA Modules:
  0.0 2537.0 jit_solution(3151116245505557041)
XLA Ops:
  7.2 6.4 collective-permute-start
  17.8 5.4 collective-permute-done.1
  26.4 9.5 collective-permute-done.2
  42.1 17.0 collective-permute-done.3
  63.5 76.1 %collective-permute-done.4 = bf16[384,2304]{1,0:T(8,128)(2,1)S(1)} collective-permute-done((bf16[384,2304]{1,0:T(8,128)(2,1)}, bf16[384,2304]{1,0:T(8,128)(2,1)S(1)}, u32[]{:S(2)}, u32[]{:S(2)}) %collective-permute-start.4) | collective-permute-done | bytes 1769504 | tf_op jit(solution)/shard_map/ppermute | solution.py:18
  146.1 6.6 fusion.177
  167.5 35.8 %all-gather.9.cloned.1.call-done = bf16[4096,768]{1,0:T(8,128)(2,1)} async-done(((bf16[1024,768]{1,0:T(8,128)(2,1)}), bf16[4096,768]{1,0:T(8,128)(2,1)}) %all-gather.9.cloned.1.call-update) | async-done | bytes 6291472 | tf_op jit(solution)/shard_map/all_gather | solution.py:108
  203.2 8.8 copy.69
  212.0 11.5 reshape.1447
  223.5 14.2 copy.91
  237.7 13.5 all-gather.7.cloned.1.call-done
  251.2 8.8 copy.68
  260.0 11.2 reshape.1445
  271.2 14.2 copy.90
  285.9 162.2 %while.64 = (s32[]{:T(128)}, bf16[12,1024,64]{1,2,0:T(8,128)(2,1)}, f32[12,1024]{1,0:T(8,128)}, s32[12]{0:T(128)}, s32[1,1024]{1,0:T(1,128)S(1)}, /*index=5*/bf1...) while((s32[]{:T(128)}, bf16[12,1024,64]{1,2,0:T(8,128)(2,1)}, ...), condition=%wide.region_23.24_spmd, body=%wide.region_2.23_spmd.sunk | while | flops 837097984 | bytes 77652256 | solution.py:166
  287.4 9.4 conditional.4
  300.1 9.4 conditional.4
  312.8 9.4 conditional.4
  325.5 9.4 conditional.4
  338.2 9.4 conditional.4
  351.0 9.4 conditional.4
  363.7 9.4 conditional.4
  376.4 9.4 conditional.4
  389.1 9.4 conditional.4
  401.8 9.4 conditional.4
  414.6 9.5 conditional.4
  427.3 9.4 conditional.4
  448.1 4.0 fusion.231
  453.0 38.3 %multiply_convert_fusion.8 = (bf16[1024,3072]{1,0:T(8,128)(2,1)}, f32[1024,3072]{1,0:T(8,128)}, f32[1024,3072]{1,0:T(8,128)}) fusion(f32[3072]{0:T(1024)S(1)} %copy-done.68, bf16[768,3072]{1,0:T(8,128)(2,1)} %all-gather.13.cloned.1.call-done, f32[1024,768]{0,1:T(8,128)S(1)} %get-tuple-element.1136, f32[768]{0:T(1024)S(1)} %copy-done.69, ...), kind=kOutput, calls=%fused_computation.371 | convolution fusion | flops 5043388416 | bytes 39348224 | tf_op jit(solution)/shard_map/dot_general | solution.py:36
  491.2 19.0 convert_reduce_fusion
  510.2 10.3 fusion.233
  533.9 450.8 %while.65 = (s32[]{:T(128)}, bf16[12,1024,64]{1,2,0:T(8,128)(2,1)}, bf16[12,4096,64]{1,2,0:T(8,128)(2,1)}, bf16[12,4096,64]{1,2,0:T(8,128)(2,1)}, s32[12]{0:T(12...) while((s32[]{:T(128)}, bf16[12,1024,64]{1,2,0:T(8,128)(2,1)}, ...), condition=%wide.region_41.42_spmd, body=%wide.region_28.41_spmd.sunk | while | flops 2081166848 | bytes 146125840 | solution.py:235
  536.2 43.4 %conditional.5 = (bf16[1,1024,64]{1,2,0:T(8,128)(2,1)}, bf16[1,4096,64]{1,2,0:T(8,128)(2,1)}, bf16[1,4096,64]{1,2,0:T(8,128)(2,1)}) conditional(s32[]{:T(128)} %get-tuple-element.1376, (s32[1,1024]{1,0:T(1,128)S(1)}, s32[]{:T(128)}, bf16[1,12,1024,64]{3,2,1,0:T(8,128)(2,1)}, bf16[1,12,4096,64]{3,2,1,0:T(8,128)(2,1)}, ...), branch_computations={%region_29.31_spmd, %region_32.34_spmd, %region_35.37_spmd, %regio... | conditional | flops 2081166848 | bytes 143756960 | solution.py:229
  586.3 30.1 %conditional.5 = (bf16[1,1024,64]{1,2,0:T(8,128)(2,1)}, bf16[1,4096,64]{1,2,0:T(8,128)(2,1)}, bf16[1,4096,64]{1,2,0:T(8,128)(2,1)}) conditional(s32[]{:T(128)} %get-tuple-element.1376, (s32[1,1024]{1,0:T(1,128)S(1)}, s32[]{:T(128)}, bf16[1,12,1024,64]{3,2,1,0:T(8,128)(2,1)}, bf16[1,12,4096,64]{3,2,1,0:T(8,128)(2,1)}, ...), branch_computations={%region_29.31_spmd, %region_32.34_spmd, %region_35.37_spmd, %regio... | conditional | flops 2081166848 | bytes 143756960 | solution.py:229
  622.3 29.8 %conditional.5 = (bf16[1,1024,64]{1,2,0:T(8,128)(2,1)}, bf16[1,4096,64]{1,2,0:T(8,128)(2,1)}, bf16[1,4096,64]{1,2,0:T(8,128)(2,1)}) conditional(s32[]{:T(128)} %get-tuple-element.1376, (s32[1,1024]{1,0:T(1,128)S(1)}, s32[]{:T(128)}, bf16[1,12,1024,64]{3,2,1,0:T(8,128)(2,1)}, bf16[1,12,4096,64]{3,2,1,0:T(8,128)(2,1)}, ...), branch_computations={%region_29.31_spmd, %region_32.34_spmd, %region_35.37_spmd, %regio... | conditional | flops 2081166848 | bytes 143756960 | solution.py:229
  658.0 29.7 %conditional.5 = (bf16[1,1024,64]{1,2,0:T(8,128)(2,1)}, bf16[1,4096,64]{1,2,0:T(8,128)(2,1)}, bf16[1,4096,64]{1,2,0:T(8,128)(2,1)}) conditional(s32[]{:T(128)} %get-tuple-element.1376, (s32[1,1024]{1,0:T(1,128)S(1)}, s32[]{:T(128)}, bf16[1,12,1024,64]{3,2,1,0:T(8,128)(2,1)}, bf16[1,12,4096,64]{3,2,1,0:T(8,128)(2,1)}, ...), branch_computations={%region_29.31_spmd, %region_32.34_spmd, %region_35.37_spmd, %regio... | conditional | flops 2081166848 | bytes 143756960 | solution.py:229
  693.6 29.8 %conditional.5 = (bf16[1,1024,64]{1,2,0:T(8,128)(2,1)}, bf16[1,4096,64]{1,2,0:T(8,128)(2,1)}, bf16[1,4096,64]{1,2,0:T(8,128)(2,1)}) conditional(s32[]{:T(128)} %get-tuple-element.1376, (s32[1,1024]{1,0:T(1,128)S(1)}, s32[]{:T(128)}, bf16[1,12,1024,64]{3,2,1,0:T(8,128)(2,1)}, bf16[1,12,4096,64]{3,2,1,0:T(8,128)(2,1)}, ...), branch_computations={%region_29.31_spmd, %region_32.34_spmd, %region_35.37_spmd, %regio... | conditional | flops 2081166848 | bytes 143756960 | solution.py:229
  729.3 29.8 %conditional.5 = (bf16[1,1024,64]{1,2,0:T(8,128)(2,1)}, bf16[1,4096,64]{1,2,0:T(8,128)(2,1)}, bf16[1,4096,64]{1,2,0:T(8,128)(2,1)}) conditional(s32[]{:T(128)} %get-tuple-element.1376, (s32[1,1024]{1,0:T(1,128)S(1)}, s32[]{:T(128)}, bf16[1,12,1024,64]{3,2,1,0:T(8,128)(2,1)}, bf16[1,12,4096,64]{3,2,1,0:T(8,128)(2,1)}, ...), branch_computations={%region_29.31_spmd, %region_32.34_spmd, %region_35.37_spmd, %regio... | conditional | flops 2081166848 | bytes 143756960 | solution.py:229
  764.9 29.7 %conditional.5 = (bf16[1,1024,64]{1,2,0:T(8,128)(2,1)}, bf16[1,4096,64]{1,2,0:T(8,128)(2,1)}, bf16[1,4096,64]{1,2,0:T(8,128)(2,1)}) conditional(s32[]{:T(128)} %get-tuple-element.1376, (s32[1,1024]{1,0:T(1,128)S(1)}, s32[]{:T(128)}, bf16[1,12,1024,64]{3,2,1,0:T(8,128)(2,1)}, bf16[1,12,4096,64]{3,2,1,0:T(8,128)(2,1)}, ...), branch_computations={%region_29.31_spmd, %region_32.34_spmd, %region_35.37_spmd, %regio... | conditional | flops 2081166848 | bytes 143756960 | solution.py:229
  800.6 29.7 %conditional.5 = (bf16[1,1024,64]{1,2,0:T(8,128)(2,1)}, bf16[1,4096,64]{1,2,0:T(8,128)(2,1)}, bf16[1,4096,64]{1,2,0:T(8,128)(2,1)}) conditional(s32[]{:T(128)} %get-tuple-element.1376, (s32[1,1024]{1,0:T(1,128)S(1)}, s32[]{:T(128)}, bf16[1,12,1024,64]{3,2,1,0:T(8,128)(2,1)}, bf16[1,12,4096,64]{3,2,1,0:T(8,128)(2,1)}, ...), branch_computations={%region_29.31_spmd, %region_32.34_spmd, %region_35.37_spmd, %regio... | conditional | flops 2081166848 | bytes 143756960 | solution.py:229
  836.3 29.7 %conditional.5 = (bf16[1,1024,64]{1,2,0:T(8,128)(2,1)}, bf16[1,4096,64]{1,2,0:T(8,128)(2,1)}, bf16[1,4096,64]{1,2,0:T(8,128)(2,1)}) conditional(s32[]{:T(128)} %get-tuple-element.1376, (s32[1,1024]{1,0:T(1,128)S(1)}, s32[]{:T(128)}, bf16[1,12,1024,64]{3,2,1,0:T(8,128)(2,1)}, bf16[1,12,4096,64]{3,2,1,0:T(8,128)(2,1)}, ...), branch_computations={%region_29.31_spmd, %region_32.34_spmd, %region_35.37_spmd, %regio... | conditional | flops 2081166848 | bytes 143756960 | solution.py:229
  872.0 29.7 %conditional.5 = (bf16[1,1024,64]{1,2,0:T(8,128)(2,1)}, bf16[1,4096,64]{1,2,0:T(8,128)(2,1)}, bf16[1,4096,64]{1,2,0:T(8,128)(2,1)}) conditional(s32[]{:T(128)} %get-tuple-element.1376, (s32[1,1024]{1,0:T(1,128)S(1)}, s32[]{:T(128)}, bf16[1,12,1024,64]{3,2,1,0:T(8,128)(2,1)}, bf16[1,12,4096,64]{3,2,1,0:T(8,128)(2,1)}, ...), branch_computations={%region_29.31_spmd, %region_32.34_spmd, %region_35.37_spmd, %regio... | conditional | flops 2081166848 | bytes 143756960 | solution.py:229
  907.7 29.7 %conditional.5 = (bf16[1,1024,64]{1,2,0:T(8,128)(2,1)}, bf16[1,4096,64]{1,2,0:T(8,128)(2,1)}, bf16[1,4096,64]{1,2,0:T(8,128)(2,1)}) conditional(s32[]{:T(128)} %get-tuple-element.1376, (s32[1,1024]{1,0:T(1,128)S(1)}, s32[]{:T(128)}, bf16[1,12,1024,64]{3,2,1,0:T(8,128)(2,1)}, bf16[1,12,4096,64]{3,2,1,0:T(8,128)(2,1)}, ...), branch_computations={%region_29.31_spmd, %region_32.34_spmd, %region_35.37_spmd, %regio... | conditional | flops 2081166848 | bytes 143756960 | solution.py:229
  943.3 29.7 %conditional.5 = (bf16[1,1024,64]{1,2,0:T(8,128)(2,1)}, bf16[1,4096,64]{1,2,0:T(8,128)(2,1)}, bf16[1,4096,64]{1,2,0:T(8,128)(2,1)}) conditional(s32[]{:T(128)} %get-tuple-element.1376, (s32[1,1024]{1,0:T(1,128)S(1)}, s32[]{:T(128)}, bf16[1,12,1024,64]{3,2,1,0:T(8,128)(2,1)}, bf16[1,12,4096,64]{3,2,1,0:T(8,128)(2,1)}, ...), branch_computations={%region_29.31_spmd, %region_32.34_spmd, %region_35.37_spmd, %regio... | conditional | flops 2081166848 | bytes 143756960 | solution.py:229
  984.7 11.2 convert_element_type.251
  995.9 9.5 copy.108
  1005.4 11.2 convert_element_type.255
  1016.6 9.5 copy.109
  1026.9 5.3 fusion.204
  1032.4 10.8 fusion.213
  1044.6 10.2 fusion.198
  1054.9 838.6 %reduce-scatter.7.cloned.1.call-done = bf16[1024,768]{0,1:T(8,128)(2,1)} async-done(((bf16[4096,768]{0,1:T(8,128)(2,1)}), bf16[1024,768]{0,1:T(8,128)(2,1)}) %reduce-scatter.7.cloned.1.call-update) | async-done | bytes 1572880 | tf_op jit(solution)/shard_map/reduce_scatter | solution.py:241
  1893.5 61.1 %reduce-scatter.9.cloned.1.call-done = bf16[1024,768]{0,1:T(8,128)(2,1)} async-done(((bf16[4096,768]{0,1:T(8,128)(2,1)}), bf16[1024,768]{0,1:T(8,128)(2,1)}) %reduce-scatter.9.cloned.1.call-update) | async-done | bytes 1572880 | tf_op jit(solution)/shard_map/reduce_scatter | solution.py:244
  1954.6 9.0 fusion.196
  1964.4 10.3 fusion.201
  1977.2 40.4 %all-gather.17.cloned.1.call-done = bf16[768,2304]{1,0:T(8,128)(2,1)} async-done(((bf16[24,2304]{1,0:T(8,128)(2,1)}), bf16[768,2304]{1,0:T(8,128)(2,1)}) %all-gather.17.cloned.1.call-update) | async-done | bytes 3538960 | tf_op jit(solution)/shard_map/all_gather | solution.py:176
  2017.6 8.5 fusion.232
  2026.1 3.5 copy.80
  2037.8 3.7 copy.84
  2041.8 40.5 %all-reduce.14 = (f32[768]{0:T(1024)}, f32[768]{0:T(1024)}, f32[768]{0:T(1024)}, f32[768]{0:T(1024)}, f32[768]{0:T(1024)}, /*index=5*/f32[768]{0:T(1024)}, f32[7...) all-reduce(f32[768]{0:T(1024)S(1)} %reduce_sum.365, ...), channel_id=1, replica_groups=mesh['seq'=8,'pass'=4] {'seq','pass'}, use_global_device_ids=true, to_apply=%region_48.49 | all-reduce | flops 12288 | bytes 98304 | tf_op jit(solution)/shard_map/psum | solution.py:276
  2082.9 38.5 %reduce-scatter.13.cloned.1.call-done = f32[24,768]{1,0:T(8,128)} async-done(((f32[768,768]{1,0:T(8,128)}), f32[24,768]{1,0:T(8,128)}) %reduce-scatter.13.cloned.1.call-update) | async-done | bytes 73744 | tf_op jit(solution)/shard_map/reduce_scatter | solution.py:261
  2121.4 141.8 %reduce-scatter.15.cloned.1.call-done = f32[24,3072]{1,0:T(8,128)} async-done(((f32[768,3072]{1,0:T(8,128)}), f32[24,3072]{1,0:T(8,128)}) %reduce-scatter.15.cloned.1.call-update) | async-done | bytes 294928 | tf_op jit(solution)/shard_map/reduce_scatter | solution.py:262
  2263.2 141.2 %reduce-scatter.17.cloned.1.call-done = f32[96,768]{1,0:T(8,128)} async-done(((f32[3072,768]{1,0:T(8,128)}), f32[96,768]{1,0:T(8,128)}) %reduce-scatter.17.cloned.1.call-update) | async-done | bytes 294928 | tf_op jit(solution)/shard_map/reduce_scatter | solution.py:263
  2404.4 125.3 %reduce-scatter.11.cloned.1.call-done = f32[24,2304]{1,0:T(8,128)} async-done(((f32[768,2304]{1,0:T(8,128)}), f32[24,2304]{1,0:T(8,128)}) %reduce-scatter.11.cloned.1.call-update) | async-done | bytes 221200 | tf_op jit(solution)/shard_map/reduce_scatter | solution.py:260
  (963 shorter events, 598.6 us)
Async XLA Ops:
  7.2 55.2 %copy-start = (f32[4,768]{1,0:T(4,128)S(1)}, f32[4,768]{1,0:T(4,128)}, u32[]{:S(2)}) copy-start(f32[4,768]{1,0:T(4,128)} %param.100) | copy-start | bytes 36868
  7.2 196.0 %all-gather.9.cloned.1.call-start = ((), (), s32[]{:S(2)}) async-start(), calls=%async_computation.7 | async-start | bytes 7864320 | tf_op jit(solution)/shard_map/all_gather | solution.py:108
  7.2 9.1 collective-permute-start
  17.2 6.0 collective-permute-start.1
  23.2 37.4 %copy-start.33 = (bf16[48,2304]{1,0:T(8,128)(2,1)}, bf16[48,2304]{1,0:T(8,128)(2,1)S(1)}, u32[]{:S(2)}) copy-start(bf16[48,2304]{1,0:T(8,128)(2,1)S(1)} %collective-permute-done.1) | copy-start | bytes 663556
  24.2 11.6 collective-permute-start.2
  35.8 24.7 copy-start.31
  36.9 22.2 collective-permute-start.3
  60.6 79.0 %collective-permute-start.4 = (bf16[384,2304]{1,0:T(8,128)(2,1)}, bf16[384,2304]{1,0:T(8,128)(2,1)S(1)}, u32[]{:S(2)}, u32[]{:S(2)}) collective-permute-start(bf16[384,2304]{1,0:T(8,128)(2,1)} %get-tuple-element.1125), channel_id=1, source_target_pairs={{0,16},{1,17},{2,18},{3,19},{4,20},{5,21},{6,22},{7,23},{8,24},{9,... | collective-permute-start | bytes 5308424 | tf_op jit(solution)/shard_map/ppermute | solution.py:18
  62.4 83.7 %copy-start.16 = (bf16[1,1024,768]{1,2,0:T(8,128)(2,1)}, bf16[1,1024,768]{1,2,0:T(8,128)(2,1)S(1)}, u32[]{:S(2)}) copy-start(bf16[1,1024,768]{1,2,0:T(8,128)(2,1)S(1)} %copy.66) | copy-start | bytes 4718596
  62.5 83.6 %copy-start.42 = (f32[768]{0:T(1024)}, f32[768]{0:T(1024)S(1)}, u32[]{:S(2)}) copy-start(f32[768]{0:T(1024)S(1)} %dynamic-slice_reduce_fusion) | copy-start | bytes 9220
  62.5 78.5 %copy-start.30 = (bf16[24,2304]{1,0:T(8,128)(2,1)S(1)}, bf16[24,2304]{1,0:T(8,128)(2,1)}, u32[]{:S(2)}) copy-start(bf16[24,2304]{1,0:T(8,128)(2,1)} %param.103) | copy-start | bytes 331780
  62.9 79.4 %copy-start.34 = (bf16[48,2304]{1,0:T(8,128)(2,1)S(1)}, bf16[48,2304]{1,0:T(8,128)(2,1)}, u32[]{:S(2)}) copy-start(bf16[48,2304]{1,0:T(8,128)(2,1)} %copy-done.33) | copy-start | bytes 663556
  62.9 80.1 %copy-start.32 = (bf16[96,2304]{1,0:T(8,128)(2,1)S(1)}, bf16[96,2304]{1,0:T(8,128)(2,1)}, u32[]{:S(2)}) copy-start(bf16[96,2304]{1,0:T(8,128)(2,1)} %copy-done.31) | copy-start | bytes 1327108
  62.9 83.2 %copy-start.45 = (f32[1024]{0:T(1024)}, f32[1024]{0:T(1024)S(1)}, u32[]{:S(2)}) copy-start(f32[1024]{0:T(1024)S(1)} %broadcast_multiply_fusion.2) | copy-start | bytes 12292
  62.9 80.8 %copy-start.36 = (bf16[192,2304]{1,0:T(8,128)(2,1)S(1)}, bf16[192,2304]{1,0:T(8,128)(2,1)}, u32[]{:S(2)}) copy-start(bf16[192,2304]{1,0:T(8,128)(2,1)} %copy-done.35) | copy-start | bytes 2654212
  63.5 78.7 %copy-start.57 = (f32[1024]{0:T(1024)}, f32[1024]{0:T(1024)S(1)}, u32[]{:S(2)}) copy-start(f32[1024]{0:T(1024)S(1)} %fusion.193) | copy-start | bytes 12292
  63.5 82.6 %copy-start.49 = (f32[1024]{0:T(1024)}, f32[1024]{0:T(1024)S(1)}, u32[]{:S(2)}) copy-start(f32[1024]{0:T(1024)S(1)} %fusion.207) | copy-start | bytes 12292
  146.1 6.6 copy-start.64
  146.1 6.6 copy-start.65
  156.9 5.4 copy-start.37
  156.9 94.3 %all-gather.7.cloned.1.call-start = ((), (), s32[]{:S(2)}) async-start(), calls=%async_computation.6 | async-start | bytes 7864320 | tf_op jit(solution)/shard_map/all_gather | solution.py:107
  160.3 287.8 %all-gather.11.cloned.1.call-start = ((), (), s32[]{:S(2)}) async-start(), calls=%async_computation.8 | async-start | bytes 1216512 | tf_op jit(solution)/shard_map/all_gather | solution.py:94
  161.0 291.6 %all-gather.13.cloned.1.call-start = ((), (), s32[]{:S(2)}) async-start(), calls=%async_computation.9 | async-start | bytes 4866048 | tf_op jit(solution)/shard_map/all_gather | solution.py:95
  161.6 329.6 %all-gather.15.cloned.1.call-start = ((), (), s32[]{:S(2)}) async-start(), calls=%async_computation.10 | async-start | bytes 4866048 | tf_op jit(solution)/shard_map/all_gather | solution.py:96
  162.2 1731.3 %reduce-scatter.7.cloned.1.call-start = ((), (), s32[]{:S(2)}) async-start(), calls=%async_computation.11 | async-start | bytes 7864320 | tf_op jit(solution)/shard_map/reduce_scatter | solution.py:241
  271.2 14.7 copy-start.25
  285.9 162.2 %copy-start.43 = (f32[768]{0:T(1024)S(1)}, f32[768]{0:T(1024)}, u32[]{:S(2)}) copy-start(f32[768]{0:T(1024)} %copy-done.42) | copy-start | bytes 9220
  452.1 76.6 %copy-start.20 = (f32[1024,768]{0,1:T(8,128)}, f32[1024,768]{0,1:T(8,128)S(1)}, u32[]{:S(2)}) copy-start(f32[1024,768]{0,1:T(8,128)S(1)} %get-tuple-element.1136) | copy-start | bytes 9437188
  452.2 76.6 %copy-start.53 = (f32[1024]{0:T(1024)}, f32[1024]{0:T(1024)S(1)}, u32[]{:S(2)}) copy-start(f32[1024]{0:T(1024)S(1)} %broadcast_multiply_fusion.1) | copy-start | bytes 12292
  452.6 76.2 %copy-start.55 = (f32[1024]{0:T(1024)}, f32[1024]{0:T(1024)S(1)}, u32[]{:S(2)}) copy-start(f32[1024]{0:T(1024)S(1)} %fusion.208) | copy-start | bytes 12292
  550.9 6.3 copy-start.13
  601.0 6.3 copy-start.13
  637.0 6.3 copy-start.13
  664.8 4.2 copy-start.9
  672.7 6.3 copy-start.13
  708.3 6.3 copy-start.13
  744.0 6.3 copy-start.13
  779.6 6.3 copy-start.13
  807.5 4.2 copy-start.9
  815.3 6.3 copy-start.13
  851.0 6.3 copy-start.13
  886.7 6.3 copy-start.13
  922.4 6.3 copy-start.13
  958.0 6.3 copy-start.13
  1005.4 949.2 %reduce-scatter.9.cloned.1.call-start = ((), (), s32[]{:S(2)}) async-start(), calls=%async_computation.12 | async-start | bytes 7864320 | tf_op jit(solution)/shard_map/reduce_scatter | solution.py:244
  1026.1 991.5 %all-gather.17.cloned.1.call-start = ((), (), s32[]{:S(2)}) async-start(), calls=%async_computation.13 | async-start | bytes 3649536 | tf_op jit(solution)/shard_map/all_gather | solution.py:176
  1026.8 5.5 copy-start.21
  1026.8 5.5 copy-start.54
  1026.9 5.5 copy-start.56
  1026.9 5.5 copy-start.60
  1026.9 5.5 copy-start.70
  1026.9 1094.5 %reduce-scatter.13.cloned.1.call-start = ((), (), s32[]{:S(2)}) async-start(), calls=%async_computation.15 | async-start | bytes 2433024 | tf_op jit(solution)/shard_map/reduce_scatter | solution.py:261
  1032.3 1230.9 %reduce-scatter.15.cloned.1.call-start = ((), (), s32[]{:S(2)}) async-start(), calls=%async_computation.16 | async-start | bytes 9732096 | tf_op jit(solution)/shard_map/reduce_scatter | solution.py:262
  1043.2 1361.2 %reduce-scatter.17.cloned.1.call-start = ((), (), s32[]{:S(2)}) async-start(), calls=%async_computation.17 | async-start | bytes 9732096 | tf_op jit(solution)/shard_map/reduce_scatter | solution.py:263
  1054.8 899.8 %copy-start.17 = (bf16[1,1024,768]{1,2,0:T(8,128)(2,1)S(1)}, bf16[1,1024,768]{1,2,0:T(8,128)(2,1)}, u32[]{:S(2)}) copy-start(bf16[1,1024,768]{1,2,0:T(8,128)(2,1)} %copy-done.16) | copy-start | bytes 4718596
  1054.8 899.8 %copy-start.39 = (bf16[12,1024,64]{1,2,0:T(8,128)(2,1)S(1)}, bf16[12,1024,64]{1,2,0:T(8,128)(2,1)}, u32[]{:S(2)}) copy-start(bf16[12,1024,64]{1,2,0:T(8,128)(2,1)} %get-tuple-element.909) | copy-start | bytes 4718596
  1054.8 899.8 %copy-start.44 = (f32[768]{0:T(1024)S(1)}, f32[768]{0:T(1024)}, u32[]{:S(2)}) copy-start(f32[768]{0:T(1024)} %copy-done.42) | copy-start | bytes 9220
  1054.8 899.8 %copy-start.46 = (f32[1024]{0:T(1024)S(1)}, f32[1024]{0:T(1024)}, u32[]{:S(2)}) copy-start(f32[1024]{0:T(1024)} %copy-done.45) | copy-start | bytes 12292
  1054.8 899.8 %copy-start.48 = (f32[768]{0:T(1024)S(1)}, f32[768]{0:T(1024)}, u32[]{:S(2)}) copy-start(f32[768]{0:T(1024)} %param.101) | copy-start | bytes 9220
  1054.8 899.8 %copy-start.50 = (f32[1024]{0:T(1024)S(1)}, f32[1024]{0:T(1024)}, u32[]{:S(2)}) copy-start(f32[1024]{0:T(1024)} %copy-done.49) | copy-start | bytes 12292
  1054.8 899.8 %copy-start.52 = (f32[768]{0:T(1024)S(1)}, f32[768]{0:T(1024)}, u32[]{:S(2)}) copy-start(f32[768]{0:T(1024)} %param.102) | copy-start | bytes 9220
  1054.8 1474.9 %reduce-scatter.11.cloned.1.call-start = ((), (), s32[]{:S(2)}) async-start(), calls=%async_computation.14 | async-start | bytes 7299072 | tf_op jit(solution)/shard_map/reduce_scatter | solution.py:260
  2037.8 492.0 %copy-start.1 = (f32[4,768]{1,0:T(4,128)S(1)}, f32[4,768]{1,0:T(4,128)}, u32[]{:S(2)}) copy-start(f32[4,768]{1,0:T(4,128)} %param.100) | copy-start | bytes 36868
  (115 other events, 264.3 us)
Sparse Core Ops, SparseCore 0:
  157.0 46.1 all-gather.8
  204.8 46.3 all-gather.6
  254.1 54.0 all-gather.10
  310.9 62.6 all-gather.12
  376.4 62.4 all-gather.14
  1005.5 887.9 reduce-scatter.6
  1896.2 58.3 reduce-scatter.8
  1957.5 60.0 all-gather.16
  2023.5 97.8 reduce-scatter.12
  2128.7 134.4 reduce-scatter.14
  2269.7 134.6 reduce-scatter.16
  2411.4 118.2 reduce-scatter.10
